TPU v7x, 128 devices: a whole 4x4x4 slice. The times are simulated.
128 devices in a mesh: row: 8 (over y, core), col: 16 (over x, z).
Axes of the slice: x: 4, y: 4, z: 4, core: 2. Of those that a mesh axis runs over, the one named last changes fastest.
Arguments:
- contribution: float32 [8, 8, 4, 16, 128, 128], P(None, 'row', None, 'col'), may hold values from -6 to 6
- parent_tiles: float32 [16, 8, 8, 16, 128, 128], P(None, 'row', None, 'col'), may hold values from -6 to 6
- row_basis: float32 [8, 8, 64, 128], P(None, 'row'), may hold values from -2.4 to 2.4
- pivot_basis: float32 [8, 8, 64, 2048], P(None, 'row', None, 'col'), may hold values from -0.125 to 0.125
- tile_ranks: int32 [64], replicated, may hold values from 16 to 64, as said below
- block_map: int32 [64], replicated, may hold values from 0 to 127, as said below
- panel_start: int32 [1], replicated, may hold values from 0 to 63
- pivot_inverse: float32 [512, 512], replicated
Outputs:
- updated_parent: float32 [16, 8, 8, 16, 128, 128], P(None, 'row', None, 'col')
Inputs may be any that keep to these rules, and one draw needn't show every extreme that they name: `tile_ranks`: multiples of 16; both 16 and 64 occur. `block_map`: child tile row u * 16 + l, for 0 <= l < 16, maps to parent tile row 2 * 16 * u + h_u + l with 0 <= h_u < 16; the 4 values h_u are distinct modulo 8.
All inputs are finite; a program needn't handle non-finite values.
Results may differ from a plain program's by a relative error of at most 0.0003.
Values sent between devices are 32-bit elements; how exact they have to be, the bound alone decides.
No kernel may reach another device: no remote copies, remote signals or barrier semaphores. Data moves between devices by JAX's collectives and lax.ppermute only.
A program may use at most 128 MiB of HBM per device.

v0:
```python
import jax
import jax.numpy as jnp
from jax import lax
from jax.sharding import PartitionSpec as P

PANEL_T = 4
highest = lax.Precision.HIGHEST


def spread_2(x, axis, root):
    mine = lax.axis_index(axis) == root
    return lax.psum(jnp.where(mine, x, jnp.zeros_like(x)), axis)


def from_behind(x, axis, by):
    count = lax.axis_size(axis)
    return lax.ppermute(x, axis, [(i, (i + by) % count) for i in range(count)])


def select_entries(lookup, wanted):
    matches = wanted[:, None] == jnp.arange(lookup.shape[0], dtype=jnp.int32)[None, :]
    return jnp.sum(jnp.where(matches, lookup[None, :], 0), axis=1)


def keep_ranks(factor, tile_index, rank_table):
    limits = select_entries(rank_table, tile_index)
    kept_cols = (jnp.arange(factor.shape[1], dtype=jnp.int32)[None, :] < limits[:, None]).astype(
        jnp.float32
    )
    return factor * kept_cols[:, :, None]


def every_other(stacked, groups, offset):
    shaped = stacked.reshape((groups, stacked.shape[0] // groups) + stacked.shape[1:])
    return lax.dynamic_index_in_dim(shaped, offset, axis=1, keepdims=False)


def per_device(
    contribution,
    parent_tiles,
    row_basis,
    pivot_basis,
    tile_ranks,
    block_map,
    panel_start,
    pivot_inverse,
):
    rows_grid = lax.axis_size("row")
    cols_grid = lax.axis_size("col")
    my_row = lax.axis_index("row")
    my_col = lax.axis_index("col")
    local_rows = contribution.shape[0]
    local_cols = contribution.shape[2]
    parent_rows = parent_tiles.shape[0]
    parent_cols = parent_tiles.shape[2]
    rank_max = row_basis.shape[2]
    per_block = cols_grid // rows_grid
    row_index = jnp.arange(local_rows, dtype=jnp.int32) * rows_grid + my_row
    col_index = jnp.arange(local_cols, dtype=jnp.int32) * cols_grid + my_col
    root_row = my_col % rows_grid
    offset = my_col // rows_grid
    own_basis = keep_ranks(row_basis[:, 0], row_index, tile_ranks)
    own_pivots = pivot_basis[:, 0]
    basis_picked = every_other(row_basis[:, 0], local_cols, offset)
    col_basis = spread_2(basis_picked, "row", root_row)
    all_pivots = lax.all_gather(pivot_basis, "row", axis=1, tiled=True)
    pivot_width = pivot_basis.shape[3]
    grouped = all_pivots.reshape(local_cols, cols_grid, rank_max, pivot_width)
    products = jnp.einsum(
        "trp,scup->cstru",
        own_pivots,
        grouped,
        precision=highest,
        preferred_element_type=jnp.float32,
    )
    weights = lax.psum_scatter(
        products.reshape(lax.axis_size("col") * local_cols, local_rows, rank_max * rank_max),
        "col",
        scatter_dimension=0,
        tiled=True,
    )
    weights = weights.reshape(local_cols, local_rows, rank_max, rank_max)
    col_basis = keep_ranks(col_basis, col_index, tile_ranks)
    half_product = jnp.einsum(
        "trx,stru->tsux", own_basis, weights, precision=highest, preferred_element_type=jnp.float32
    )
    update = jnp.einsum(
        "tsux,suy->tsxy",
        half_product,
        col_basis,
        precision=highest,
        preferred_element_type=jnp.float32,
    )
    lower_mask = (row_index[:, None] >= col_index[None, :])[:, :, None, None]
    payload = jnp.where(lower_mask, contribution[:, 0, :, 0] - update, jnp.float32(0.0))
    block_first = jnp.arange(local_cols, dtype=jnp.int32) * cols_grid
    shifts = select_entries(block_map, block_first) - 2 * block_first
    row_shift = jnp.repeat(shifts, per_block) % rows_grid
    for bit_index in range((rows_grid - 1).bit_length()):
        arrived = from_behind(payload, "row", 1 << bit_index)
        taken = row_shift // (1 << bit_index) % 2 == 1
        payload = jnp.where(taken[:, None, None, None], arrived, payload)
    for bit_index in range((cols_grid - 1).bit_length()):
        arrived = from_behind(payload, "col", 1 << bit_index)
        taken = shifts // (1 << bit_index) % 2 == 1
        payload = jnp.where(taken[None, :, None, None], arrived, payload)
    row_source = (my_row - row_shift) % rows_grid
    target_rows = (
        select_entries(block_map, jnp.arange(local_rows, dtype=jnp.int32) * rows_grid + row_source)
        // rows_grid
    )
    col_source = (my_col - shifts) % cols_grid
    target_cols = (
        select_entries(block_map, jnp.arange(local_cols, dtype=jnp.int32) * cols_grid + col_source)
        // cols_grid
    )
    row_place = (jnp.arange(parent_rows, dtype=jnp.int32)[:, None] == target_rows[None, :]).astype(
        jnp.float32
    )
    col_place = (jnp.arange(parent_cols, dtype=jnp.int32)[:, None] == target_cols[None, :]).astype(
        jnp.float32
    )
    spread = jnp.einsum(
        "at,tsxy->asxy", row_place, payload, precision=highest, preferred_element_type=jnp.float32
    )
    spread = jnp.einsum(
        "bs,asxy->abxy", col_place, spread, precision=highest, preferred_element_type=jnp.float32
    )
    assembled = parent_tiles[:, 0, :, 0] + spread
    start_col = panel_start[0]
    panel_parts = []
    for panel_index in range(PANEL_T):
        column_id = start_col + panel_index
        column = lax.dynamic_index_in_dim(assembled, column_id // cols_grid, axis=1, keepdims=False)
        panel_parts.append(spread_2(column, "col", column_id % cols_grid))
    row_panel = jnp.concatenate(panel_parts, axis=2)
    col_panel = spread_2(every_other(row_panel, parent_cols, offset), "row", root_row)
    scaled = jnp.einsum(
        "axp,pq->axq",
        row_panel,
        pivot_inverse,
        precision=highest,
        preferred_element_type=jnp.float32,
    )
    trailing = jnp.einsum(
        "axq,byq->abxy", scaled, col_panel, precision=highest, preferred_element_type=jnp.float32
    )
    big_rows = jnp.arange(parent_rows, dtype=jnp.int32) * rows_grid + my_row
    big_cols = jnp.arange(parent_cols, dtype=jnp.int32) * cols_grid + my_col
    window = (big_rows[:, None] >= big_cols[None, :]) & (big_cols[None, :] >= start_col + PANEL_T)
    result = jnp.where(window[:, :, None, None], assembled - trailing, assembled)
    return result[:, None, :, None]


def solution(mesh):
    placed = (
        P(None, "row", None, "col", None, None),
        P(None, "row", None, "col", None, None),
        P(None, "row", None, None),
        P(None, "row", None, "col"),
        P(),
        P(),
        P(),
        P(),
    )
    return jax.shard_map(
        per_device,
        mesh=mesh,
        in_specs=placed,
        out_specs=P(None, "row", None, "col", None, None),
        check_vma=False,
    )
```

profile of v0, /device:TPU:0, one launch (start us, length us, event | category | flops | bytes accessed | tf_op | source)
XLA Modules:
  0.0 810.4 jit_solution(2350074608308215927)
XLA Ops:
  6.5 0.7 all-gather.2.cloned.1.call-update
  7.3 29.4 %all-gather.2.cloned.1.call-done = f32[8,8,64,128]{3,2,1,0:T(8,128)} async-done(((f32[8,1,64,128]{3,2,1,0:T(8,128)}), f32[8,8,64,128]{3,2,1,0:T(8,128)}) %all-gather.2.cloned.1.call-update) | async-done | bytes 2097168 | tf_op jit(solution)/shard_map/all_gather | solution.py:66
  36.7 17.0 %convolution_bitcast_fusion = f32[16,4,8,64,64]{3,4,2,0,1:T(8,128)} fusion(f32[4,16,64,128,1]{3,2,4,1,0:T(8,128)} %bitcast.109, f32[8,1,64,128]{3,2,1,0:T(8,128)} %param.11), kind=kOutput, calls=%fused_computation.1 | convolution fusion | flops 3221225472 | bytes 10747904 | tf_op jit(solution)/shard_map/trp,scup->cstru/dot_general | solution.py:69
  53.7 17.6 %copy.33 = f32[16,4,8,64,64]{4,3,2,1,0:T(8,128)} copy(f32[16,4,8,64,64]{3,4,2,0,1:T(8,128)} %convolution_bitcast_fusion) | data formatting | bytes 16777216 | tf_op jit(solution)/shard_map/trp,scup->cstru/transpose | solution.py:69
  71.3 14.7 %reshape.468 = f32[64,8,4096]{2,1,0:T(8,128)} reshape(f32[16,4,8,64,64]{4,3,2,1,0:T(8,128)} %copy.33) | data formatting | bytes 16777216 | tf_op jit(solution)/shard_map/reshape | solution.py:77
  86.2 0.8 copy-done.7
  87.0 0.7 fusion.15
  87.8 0.1 broadcast_compare_fusion
  87.9 0.2 select_reduce_fusion.3
  88.1 0.2 select_reduce_fusion
  88.4 1.8 copy.31
  90.2 81.4 %reduce-scatter.2.cloned.1.call-done = f32[4,8,4096]{2,1,0:T(8,128)} async-done(((f32[64,8,4096]{2,1,0:T(8,128)}), f32[4,8,4096]{2,1,0:T(8,128)}) %reduce-scatter.2.cloned.1.call-update) | async-done | bytes 524304 | tf_op jit(solution)/shard_map/reduce_scatter | solution.py:76
  171.7 1.5 reshape.469
  173.1 2.9 fusion.13
  176.0 56.6 %all-reduce.5.cloned.1.call-done = f32[4,64,128]{2,1,0:T(8,128)} async-done(((f32[4,64,128]{2,1,0:T(8,128)}), f32[4,64,128]{2,1,0:T(8,128)}) %all-reduce.5.cloned.1.call-update) | async-done | bytes 131088 | tf_op jit(solution)/shard_map/psum | solution.py:12
  232.6 3.9 fusion.9
  236.6 0.2 select_reduce_fusion.4
  236.9 0.1 reshape.466
  237.0 26.3 %collective-permute-done = f32[8,4,128,128]{2,3,0,1:T(8,128)} collective-permute-done((f32[8,4,128,128]{2,3,0,1:T(8,128)S(1)}, f32[8,4,128,128]{2,3,0,1:T(8,128)}, u32[]{:S(2)}, u32[]{:S(2)}) %collective-permute-start) | collective-permute-done | bytes 2097184 | tf_op jit(solution)/shard_map/ppermute | solution.py:17
  263.4 1.9 broadcast_select_fusion.1
  265.3 0.1 collective-permute-start.1
  265.3 45.3 %collective-permute-done.1 = f32[8,4,128,128]{2,3,0,1:T(8,128)S(1)} collective-permute-done((f32[8,4,128,128]{2,3,0,1:T(8,128)S(1)}, f32[8,4,128,128]{2,3,0,1:T(8,128)S(1)}, u32[]{:S(2)}, u32[]{:S(2)}) %collective-permute-start.1) | collective-permute-done | bytes 2097184 | tf_op jit(solution)/shard_map/ppermute | solution.py:17
  310.7 0.4 broadcast_select_fusion.2
  311.1 0.8 collective-permute-start.2
  311.9 45.3 %collective-permute-done.2 = f32[8,4,128,128]{2,3,0,1:T(8,128)S(1)} collective-permute-done((f32[8,4,128,128]{2,3,0,1:T(8,128)S(1)}, f32[8,4,128,128]{2,3,0,1:T(8,128)S(1)}, u32[]{:S(2)}, u32[]{:S(2)}) %collective-permute-start.2) | collective-permute-done | bytes 2097184 | tf_op jit(solution)/shard_map/ppermute | solution.py:17
  357.2 0.4 broadcast_select_fusion.3
  357.6 2.1 collective-permute-start.3
  359.7 47.1 %collective-permute-done.3 = f32[8,4,128,128]{2,3,0,1:T(8,128)S(1)} collective-permute-done((f32[8,4,128,128]{2,3,0,1:T(8,128)S(1)}, f32[8,4,128,128]{2,3,0,1:T(8,128)S(1)}, u32[]{:S(2)}, u32[]{:S(2)}) %collective-permute-start.3) | collective-permute-done | bytes 2097184 | tf_op jit(solution)/shard_map/ppermute | solution.py:17
  406.8 0.4 broadcast_select_fusion.4
  407.2 0.1 collective-permute-start.4
  407.3 49.8 %collective-permute-done.4 = f32[8,4,128,128]{2,3,0,1:T(8,128)S(1)} collective-permute-done((f32[8,4,128,128]{2,3,0,1:T(8,128)S(1)}, f32[8,4,128,128]{2,3,0,1:T(8,128)S(1)}, u32[]{:S(2)}, u32[]{:S(2)}) %collective-permute-start.4) | collective-permute-done | bytes 2097184 | tf_op jit(solution)/shard_map/ppermute | solution.py:17
  457.1 0.4 broadcast_select_fusion.5
  457.5 0.1 collective-permute-start.5
  457.6 65.4 %collective-permute-done.5 = f32[8,4,128,128]{2,3,0,1:T(8,128)S(1)} collective-permute-done((f32[8,4,128,128]{2,3,0,1:T(8,128)S(1)}, f32[8,4,128,128]{2,3,0,1:T(8,128)S(1)}, u32[]{:S(2)}, u32[]{:S(2)}) %collective-permute-start.5) | collective-permute-done | bytes 2097184 | tf_op jit(solution)/shard_map/ppermute | solution.py:17
  522.9 0.3 broadcast_select_fusion.6
  523.3 0.1 collective-permute-start.6
  524.1 0.2 select_reduce_fusion.1
  524.3 0.2 select_reduce_fusion.2
  524.5 26.5 %collective-permute-done.6 = f32[8,4,128,128]{2,3,0,1:T(8,128)} collective-permute-done((f32[8,4,128,128]{2,3,0,1:T(8,128)S(1)}, f32[8,4,128,128]{2,3,0,1:T(8,128)}, u32[]{:S(2)}, u32[]{:S(2)}) %collective-permute-start.6) | collective-permute-done | bytes 2097184 | tf_op jit(solution)/shard_map/ppermute | solution.py:17
  551.0 3.2 broadcast_select_fusion.7
  554.2 2.0 copy.35
  556.3 1.9 fusion.21
  558.2 13.0 %bitcast_add_fusion = f32[16,8,128,128]{3,1,2,0:T(8,128)S(1)} fusion(f32[16,1,8,1,128,128]{5,4,3,2,1,0:T(8,128)} %param.9, f32[16,4,128,128]{3,0,2,1:T(8,128)S(1)} %fusion.21, s32[4]{0:T(128)S(1)} %and_select_fusion), kind=kOutput, calls=%fused_computation.3 | convolution fusion | flops 102760480 | bytes 20971536 | tf_op jit(solution)/shard_map/bs,asxy->abxy/dot_general | solution.py:126
  571.2 1.2 broadcast.768
  572.4 5.8 broadcast_select_fusion
  578.2 1.1 select_bitcast_fusion.2
  579.3 1.6 select_bitcast_fusion
  580.9 0.2 all-reduce.7.cloned.1.call-start
  581.1 104.7 %all-reduce.9.cloned.1.call-done = (f32[16,128,128]{2,1,0:T(8,128)}, f32[16,128,128]{2,1,0:T(8,128)}, f32[16,128,128]{2,1,0:T(8,128)}, f32[16,128,128]{2,1,0:T(8,128)}) async-done(((f32[16,128,128]{2,1,0:T(8,128)}, f32[16,128,128]{2,1,0:T(8,128)}, f32[16,128,128]{2,1,0:T(8,128)}, f32[16,128,128]{2,1,0:T(8,128)}), (f32[16,128,128]{2,1,0:T(8,128)}, f32[16,128,128]{2,1,0:T(8,128)}, f32[16,128,128]{2,1,0:T(8,128)}, ...) | async-done | bytes 4194320 | tf_op jit(solution)/shard_map/psum | solution.py:12
  685.8 1.5 constant_dynamic-update-slice_fusion.3
  687.4 0.1 constant_dynamic-update-slice_fusion.2
  687.5 0.2 copy-done.5
  687.7 0.1 constant_dynamic-update-slice_fusion.1
  687.8 0.9 copy-done.4
  688.7 0.1 constant_dynamic-update-slice_fusion
  688.8 1.9 copy-done.2
  690.8 1.6 fusion.7
  692.4 0.1 compare_and_fusion
  692.5 9.9 %fusion.10 = f32[16,128,512]{2,1,0:T(8,128)} fusion(f32[16,128,512]{2,1,0:T(8,128)} %copy-done.2, f32[512,512]{1,0:T(8,128)S(1)} %copy-done), kind=kOutput, calls=%fused_computation.14 | convolution fusion | flops 6442450944 | bytes 9437184 | tf_op jit(solution)/shard_map/axp,pq->axq/dot_general | solution.py:138
  702.4 55.5 %all-reduce.7.cloned.1.call-done = f32[8,128,512]{2,1,0:T(8,128)} async-done(((f32[8,128,512]{2,1,0:T(8,128)}), f32[8,128,512]{2,1,0:T(8,128)}) %all-reduce.7.cloned.1.call-update) | async-done | bytes 2097168 | tf_op jit(solution)/shard_map/psum | solution.py:12
  757.9 18.0 %fusion.1 = f32[8,128,16,128]{3,1,2,0:T(8,128)} fusion(f32[16,128,512]{2,1,0:T(8,128)} %fusion.10, f32[8,128,512]{2,1,0:T(8,128)} %all-reduce.7.cloned.1.call-done), kind=kOutput, calls=%fused_computation.4 | convolution fusion | flops 12884901888 | bytes 14680064 | tf_op jit(solution)/shard_map/axq,byq->abxy/dot_general | solution.py:145
  775.9 9.4 %copy.42 = f32[8,128,16,128]{1,0,3,2:T(8,128)} copy(f32[8,128,16,128]{3,1,2,0:T(8,128)} %fusion.1) | data formatting | bytes 16777216 | tf_op jit(solution)/shard_map/axq,byq->abxy/dot_general | solution.py:145
  785.3 10.2 %fusion = f32[16,1,8,1,128,128]{5,2,4,0,3,1:T(8,128)} fusion(f32[16,8,128,128]{3,1,2,0:T(8,128)} %copy-done.1, f32[8,128,16,128]{1,0,3,2:T(8,128)} %copy.42, pred[16,8]{1,0:T(8,128)(4,1)S(1)} %compare_and_fusion), kind=kLoop, calls=%fused_computation.2 | loop fusion | flops 4194304 | bytes 25165952 | tf_op jit(solution)/shard_map/broadcast_in_dim | solution.py:152
  795.4 8.2 %copy.43 = f32[16,1,8,1,128,128]{5,4,3,2,1,0:T(8,128)} copy(f32[16,1,8,1,128,128]{5,2,4,0,3,1:T(8,128)} %fusion) | data formatting | bytes 16777216 | tf_op jit(solution)/shard_map/broadcast_in_dim | solution.py:152
  (40 shorter events, 0.6 us)
Async XLA Ops:
  6.5 686.0 %copy-start = (f32[512,512]{1,0:T(8,128)S(1)}, f32[512,512]{1,0:T(8,128)}, u32[]{:S(2)}) copy-start(f32[512,512]{1,0:T(8,128)} %param.15) | copy-start | bytes 3145732
  6.5 30.2 %all-gather.2.cloned.1.call-start = ((), (), s32[]{:S(2)}) async-start(), calls=%async_computation.2 | async-start | bytes 2359296 | tf_op jit(solution)/shard_map/all_gather | solution.py:66
  7.3 164.4 %reduce-scatter.2.cloned.1.call-start = ((), (), s32[]{:S(2)}) async-start(), calls=%async_computation.3 | async-start | bytes 8912896 | tf_op jit(solution)/shard_map/reduce_scatter | solution.py:76
  86.1 0.9 copy-start.7
  86.1 1.8 copy-start.8
  86.1 2.3 copy-start.3
  86.1 146.5 %all-reduce.5.cloned.1.call-start = ((), (), s32[]{:S(2)}) async-start(), calls=%async_computation.1 | async-start | bytes 262144 | tf_op jit(solution)/shard_map/psum | solution.py:12
  87.7 598.1 %all-reduce.9.cloned.1.call-start = ((), (), s32[]{:S(2)}) async-start(), calls=%async_computation.5 | async-start | bytes 8388608 | tf_op jit(solution)/shard_map/psum | solution.py:12
  176.0 60.6 %copy-start.9 = (s32[64]{0:T(128)S(1)}, s32[64]{0:T(128)}, u32[]{:S(2)}) copy-start(s32[64]{0:T(128)} %param.13) | copy-start | bytes 772
  236.6 26.8 %collective-permute-start = (f32[8,4,128,128]{2,3,0,1:T(8,128)S(1)}, f32[8,4,128,128]{2,3,0,1:T(8,128)}, u32[]{:S(2)}, u32[]{:S(2)}) collective-permute-start(f32[8,4,128,128]{2,3,0,1:T(8,128)S(1)} %fusion.9), channel_id=1, source_target_pairs={{0,16},{16,32},{32,48},{48,64},{64,80},{80,96},{96,112},{112,0},{1... | collective-permute-start | bytes 6291464 | tf_op jit(solution)/shard_map/ppermute | solution.py:17
  265.3 45.4 %collective-permute-start.1 = (f32[8,4,128,128]{2,3,0,1:T(8,128)S(1)}, f32[8,4,128,128]{2,3,0,1:T(8,128)S(1)}, u32[]{:S(2)}, u32[]{:S(2)}) collective-permute-start(f32[8,4,128,128]{2,3,0,1:T(8,128)S(1)} %broadcast_select_fusion.1), channel_id=1, source_target_pairs={{0,32},{16,48},{32,64},{48,80},{64,96},{80,112},{96,0},{112,16},{1... | collective-permute-start | bytes 6291464 | tf_op jit(solution)/shard_map/ppermute | solution.py:17
  311.1 46.1 %collective-permute-start.2 = (f32[8,4,128,128]{2,3,0,1:T(8,128)S(1)}, f32[8,4,128,128]{2,3,0,1:T(8,128)S(1)}, u32[]{:S(2)}, u32[]{:S(2)}) collective-permute-start(f32[8,4,128,128]{2,3,0,1:T(8,128)S(1)} %broadcast_select_fusion.2), channel_id=1, source_target_pairs={{0,64},{16,80},{32,96},{48,112},{64,0},{80,16},{96,32},{112,48},{1... | collective-permute-start | bytes 6291464 | tf_op jit(solution)/shard_map/ppermute | solution.py:17
  357.6 49.2 %collective-permute-start.3 = (f32[8,4,128,128]{2,3,0,1:T(8,128)S(1)}, f32[8,4,128,128]{2,3,0,1:T(8,128)S(1)}, u32[]{:S(2)}, u32[]{:S(2)}) collective-permute-start(f32[8,4,128,128]{2,3,0,1:T(8,128)S(1)} %broadcast_select_fusion.3), channel_id=1, source_target_pairs={{0,1},{1,2},{2,3},{3,4},{4,5},{5,6},{6,7},{7,8},{8,9},{9,10},{10,1... | collective-permute-start | bytes 6291464 | tf_op jit(solution)/shard_map/ppermute | solution.py:17
  407.2 49.9 %collective-permute-start.4 = (f32[8,4,128,128]{2,3,0,1:T(8,128)S(1)}, f32[8,4,128,128]{2,3,0,1:T(8,128)S(1)}, u32[]{:S(2)}, u32[]{:S(2)}) collective-permute-start(f32[8,4,128,128]{2,3,0,1:T(8,128)S(1)} %broadcast_select_fusion.4), channel_id=1, source_target_pairs={{0,2},{1,3},{2,4},{3,5},{4,6},{5,7},{6,8},{7,9},{8,10},{9,11},{10,... | collective-permute-start | bytes 6291464 | tf_op jit(solution)/shard_map/ppermute | solution.py:17
  457.5 65.5 %collective-permute-start.5 = (f32[8,4,128,128]{2,3,0,1:T(8,128)S(1)}, f32[8,4,128,128]{2,3,0,1:T(8,128)S(1)}, u32[]{:S(2)}, u32[]{:S(2)}) collective-permute-start(f32[8,4,128,128]{2,3,0,1:T(8,128)S(1)} %broadcast_select_fusion.5), channel_id=1, source_target_pairs={{0,4},{1,5},{2,6},{3,7},{4,8},{5,9},{6,10},{7,11},{8,12},{9,13},{1... | collective-permute-start | bytes 6291464 | tf_op jit(solution)/shard_map/ppermute | solution.py:17
  523.3 27.7 %collective-permute-start.6 = (f32[8,4,128,128]{2,3,0,1:T(8,128)S(1)}, f32[8,4,128,128]{2,3,0,1:T(8,128)}, u32[]{:S(2)}, u32[]{:S(2)}) collective-permute-start(f32[8,4,128,128]{2,3,0,1:T(8,128)S(1)} %broadcast_select_fusion.6), channel_id=1, source_target_pairs={{0,8},{1,9},{2,10},{3,11},{4,12},{5,13},{6,14},{7,15},{8,0},{9,1},... | collective-permute-start | bytes 6291464 | tf_op jit(solution)/shard_map/ppermute | solution.py:17
  571.2 7.0 copy-start.1
  580.9 177.0 %all-reduce.7.cloned.1.call-start = ((), (), s32[]{:S(2)}) async-start(), calls=%async_computation.4 | async-start | bytes 4194304 | tf_op jit(solution)/shard_map/psum | solution.py:12
  685.8 1.5 copy-start.6
  685.8 1.9 copy-start.5
  687.4 1.3 copy-start.4
  688.8 2.0 copy-start.2
Sparse Core Ops, SparseCore 0:
  9.1 27.6 all-gather.1
  86.2 85.3 reduce-scatter.1
  174.0 58.6 all-reduce.4
  581.0 104.7 all-reduce.8
  692.5 65.3 all-reduce.6
where the time goes:
time: 820 us; the launch traced here: 810 us
  waiting for transfers between devices  634 us (77%)
  matrix products  66.6 us (8%)
  local copies, waits for them, and re-layouts  62.5 us (8%)
  other arithmetic  29.3 us (4%)
  between operations  14.4 us (2%)
    ppermute x7, waiting for transfers between devices, from_behind(): return lax.ppermute(x, axis, [(i, (i + by) % count) for i in range(count)])  306 us
    psum x3, waiting for transfers between devices, spread_2(): return lax.psum(jnp.where(mine, x, jnp.zeros_like(x)), axis)  217 us
    reduce_scatter x1, waiting for transfers between devices, per_device(): lax.psum_scatter(products.reshape(lax.axis_size('col') * local_cols, loca...  81.4 us
    all_gather x1, waiting for transfers between devices, per_device(): all_pivots = lax.all_gather(pivot_basis, 'row', axis=1, tiled=True)  29.4 us
    dot_general x1, matrix products, per_device(): jnp.einsum('axq,byq->abxy', scaled, col_panel, precision=highest, preferr...  18 us
    transpose x1, local copies, waits for them, and re-layouts, per_device(): jnp.einsum('trp,scup->cstru', own_pivots, grouped, precision=highest, pre...  17.6 us
    dot_general x1, matrix products, per_device(): jnp.einsum('trp,scup->cstru', own_pivots, grouped, precision=highest, pre...  17 us
  transfers between devices with their start and end apart: 12, of which 12 were waited for; matrix products, arithmetic and copies ran while one was open for 2% of the time, Pallas kernels for 0%

commit v1 on v0

--- a/solution.py
+++ b/solution.py
@@ -2,6 +2,7 @@
 import jax.numpy as jnp
 from jax import lax
 from jax.sharding import PartitionSpec as P
+from jax.lax import axis_index, axis_size, ppermute
 
 PANEL_T = 4
 highest = lax.Precision.HIGHEST
@@ -63,7 +64,37 @@
     own_pivots = pivot_basis[:, 0]
     basis_picked = every_other(row_basis[:, 0], local_cols, offset)
     col_basis = spread_2(basis_picked, "row", root_row)
-    all_pivots = lax.all_gather(pivot_basis, "row", axis=1, tiled=True)
+
+    def unite_strings(work_x):
+        reply = axis_size("row")
+        value_now = axis_index("row")
+        current_arr, carry_out, piece_now = (reply, value_now, work_x.shape[1])
+        crops = [h * current_arr if idx == 1 else h for idx, h in enumerate(work_x.shape)]
+        lower = all_values = work_x
+        h_now = lax.dynamic_update_slice_in_dim(
+            jnp.zeros(crops, work_x.dtype), work_x, carry_out * piece_now, axis=1
+        )
+        for pp in range(1, current_arr // 2 + 1):
+            lower = ppermute(
+                lower,
+                axis_name="row",
+                perm=[(idx, (idx + 1) % current_arr) for idx in range(current_arr)],
+            )
+            h_now = lax.dynamic_update_slice_in_dim(
+                h_now, lower, (carry_out - pp) % current_arr * piece_now, axis=1
+            )
+            if 2 * pp < current_arr:
+                all_values = ppermute(
+                    all_values,
+                    "row",
+                    perm=[(idx, (idx - 1) % current_arr) for idx in range(current_arr)],
+                )
+                h_now = lax.dynamic_update_slice_in_dim(
+                    h_now, all_values, (carry_out + pp) % current_arr * piece_now, axis=1
+                )
+        return h_now
+
+    all_pivots = unite_strings(pivot_basis)
     pivot_width = pivot_basis.shape[3]
     grouped = all_pivots.reshape(local_cols, cols_grid, rank_max, pivot_width)
     products = jnp.einsum(

time: 820 us -> 756 us (0.922)
  waiting for transfers between devices: 634 us -> 555 us
  starting transfers between devices: 3.56 us -> 13.8 us
    psum x3, waiting for transfers between devices: 217 us -> 159 us  [spread_2(): return lax.psum(jnp.where(mine, x, jnp.zeros_like(x)), axis)]
    all_gather x1 -> x0, waiting for transfers between devices: 29.4 us -> none  [per_device(): all_pivots = lax.all_gather(pivot_basis, 'row', axis=1, tiled=True)]
    ppermute x0 -> x7, waiting for transfers between devices: none -> 15.6 us  [the longest x4 14.7 us: unite_strings(): ppermute(lower, axis_name='row', perm=[(idx, (idx + 1) % current_arr) for...]
    ppermute x0 -> x7, starting transfers between devices: none -> 8.88 us  [the longest x3 8.87 us: unite_strings(): ppermute(all_values, 'row', perm=[(idx, (idx - 1) % current_arr) for idx...]
  transfers between devices with their start and end apart: 12 -> 18, of which waited for: 12 -> 15; matrix products, arithmetic and copies ran while one was open for 2% -> 3% of each run, Pallas kernels for 0% -> 0%
where the time goes in v1:
time: 756 us; the launch traced here: 747 us
  waiting for transfers between devices  555 us (73%)
  local copies, waits for them, and re-layouts  66.8 us (9%)
  matrix products  65.4 us (9%)
  other arithmetic  29.4 us (4%)
  between operations  16.4 us (2%)
  starting transfers between devices  13.8 us (2%)
    ppermute x7, waiting for transfers between devices, from_behind(): return lax.ppermute(x, axis, [(i, (i + by) % count) for i in range(count)])  299 us
    psum x3, waiting for transfers between devices, spread_2(): return lax.psum(jnp.where(mine, x, jnp.zeros_like(x)), axis)  159 us
    reduce_scatter x1, waiting for transfers between devices, per_device(): lax.psum_scatter(products.reshape(lax.axis_size('col') * local_cols, loca...  80.8 us
    dot_general x1, matrix products, per_device(): jnp.einsum('axq,byq->abxy', scaled, col_panel, precision=highest, preferr...  18 us
    transpose x1, local copies, waits for them, and re-layouts, per_device(): jnp.einsum('trp,scup->cstru', own_pivots, grouped, precision=highest, pre...  17.7 us
    dot_general x1, matrix products, per_device(): jnp.einsum('trp,scup->cstru', own_pivots, grouped, precision=highest, pre...  15.8 us
  transfers between devices with their start and end apart: 18, of which 15 were waited for; matrix products, arithmetic and copies ran while one was open for 3% of the time, Pallas kernels for 0%

profile of v1, /device:TPU:0, one launch (start us, length us, event | category | flops | bytes accessed | tf_op | source)
XLA Modules:
  0.0 746.7 jit_solution(4988780816553582456)
XLA Ops:
  7.4 2.9 collective-permute-start.1
  10.3 4.4 collective-permute-done
  14.7 3.0 collective-permute-start.3
  17.7 0.2 broadcast_in_dim.171
  18.1 4.0 collective-permute-done.2
  22.0 1.0 constant_dynamic-update-slice_fusion.10
  23.0 1.0 constant_dynamic-update-slice_fusion.9
  24.0 3.0 collective-permute-start.5
  27.0 1.0 constant_dynamic-update-slice_fusion.8
  27.9 1.3 collective-permute-done.4
  29.2 1.0 constant_dynamic-update-slice_fusion.7
  30.2 0.9 collective-permute-done.5
  31.2 5.1 collective-permute-done.6
  36.3 15.8 %convolution_bitcast_fusion = f32[16,4,8,64,64]{3,4,2,0,1:T(8,128)} fusion(f32[4,16,64,128,1]{3,2,4,1,0:T(8,128)S(1)} %bitcast.104, f32[8,1,64,128]{3,2,1,0:T(8,128)S(1)} %copy-done.4), kind=kOutput, calls=%fused_computation.1 | convolution fusion | flops 3221225472 | bytes 10747904 | tf_op jit(solution)/shard_map/trp,scup->cstru/dot_general | solution.py:100
  52.1 17.7 %copy.33 = f32[16,4,8,64,64]{4,3,2,1,0:T(8,128)} copy(f32[16,4,8,64,64]{3,4,2,0,1:T(8,128)} %convolution_bitcast_fusion) | data formatting | bytes 16777216 | tf_op jit(solution)/shard_map/trp,scup->cstru/transpose | solution.py:100
  69.7 14.7 %reshape.468 = f32[64,8,4096]{2,1,0:T(8,128)} reshape(f32[16,4,8,64,64]{4,3,2,1,0:T(8,128)} %copy.33) | data formatting | bytes 16777216 | tf_op jit(solution)/shard_map/reshape | solution.py:108
  84.6 0.8 copy-done.8
  85.4 0.7 fusion.15
  86.2 0.2 select_reduce_fusion
  86.5 0.2 select_reduce_fusion.3
  86.8 1.8 copy.31
  88.6 80.8 %reduce-scatter.2.cloned.1.call-done = f32[4,8,4096]{2,1,0:T(8,128)} async-done(((f32[64,8,4096]{2,1,0:T(8,128)}), f32[4,8,4096]{2,1,0:T(8,128)}) %reduce-scatter.2.cloned.1.call-update) | async-done | bytes 524304 | tf_op jit(solution)/shard_map/reduce_scatter | solution.py:107
  169.5 1.5 reshape.469
  170.9 2.9 fusion.13
  173.8 3.9 fusion.9
  177.8 0.2 select_reduce_fusion.4
  178.2 26.3 %collective-permute-done.7 = f32[8,4,128,128]{2,3,0,1:T(8,128)} collective-permute-done((f32[8,4,128,128]{2,3,0,1:T(8,128)S(1)}, f32[8,4,128,128]{2,3,0,1:T(8,128)}, u32[]{:S(2)}, u32[]{:S(2)}) %collective-permute-start.7) | collective-permute-done | bytes 2097184 | tf_op jit(solution)/shard_map/ppermute | solution.py:18
  204.5 1.9 broadcast_select_fusion.1
  206.4 0.4 collective-permute-start.8
  206.8 46.3 %collective-permute-done.8 = f32[8,4,128,128]{2,3,0,1:T(8,128)S(1)} collective-permute-done((f32[8,4,128,128]{2,3,0,1:T(8,128)S(1)}, f32[8,4,128,128]{2,3,0,1:T(8,128)S(1)}, u32[]{:S(2)}, u32[]{:S(2)}) %collective-permute-start.8) | collective-permute-done | bytes 2097184 | tf_op jit(solution)/shard_map/ppermute | solution.py:18
  253.1 0.4 broadcast_select_fusion.2
  253.5 2.0 collective-permute-start.9
  255.5 44.5 %collective-permute-done.9 = f32[8,4,128,128]{2,3,0,1:T(8,128)S(1)} collective-permute-done((f32[8,4,128,128]{2,3,0,1:T(8,128)S(1)}, f32[8,4,128,128]{2,3,0,1:T(8,128)S(1)}, u32[]{:S(2)}, u32[]{:S(2)}) %collective-permute-start.9) | collective-permute-done | bytes 2097184 | tf_op jit(solution)/shard_map/ppermute | solution.py:18
  300.0 0.4 broadcast_select_fusion.3
  300.4 1.5 collective-permute-start.10
  301.9 46.2 %collective-permute-done.10 = f32[8,4,128,128]{2,3,0,1:T(8,128)S(1)} collective-permute-done((f32[8,4,128,128]{2,3,0,1:T(8,128)S(1)}, f32[8,4,128,128]{2,3,0,1:T(8,128)S(1)}, u32[]{:S(2)}, u32[]{:S(2)}) %collective-permute-start.10) | collective-permute-done | bytes 2097184 | tf_op jit(solution)/shard_map/ppermute | solution.py:18
  348.1 0.4 broadcast_select_fusion.4
  348.6 49.8 %collective-permute-done.11 = f32[8,4,128,128]{2,3,0,1:T(8,128)S(1)} collective-permute-done((f32[8,4,128,128]{2,3,0,1:T(8,128)S(1)}, f32[8,4,128,128]{2,3,0,1:T(8,128)S(1)}, u32[]{:S(2)}, u32[]{:S(2)}) %collective-permute-start.11) | collective-permute-done | bytes 2097184 | tf_op jit(solution)/shard_map/ppermute | solution.py:18
  398.4 0.4 broadcast_select_fusion.5
  398.9 0.5 collective-permute-start.12
  399.3 59.6 %collective-permute-done.12 = f32[8,4,128,128]{2,3,0,1:T(8,128)S(1)} collective-permute-done((f32[8,4,128,128]{2,3,0,1:T(8,128)S(1)}, f32[8,4,128,128]{2,3,0,1:T(8,128)S(1)}, u32[]{:S(2)}, u32[]{:S(2)}) %collective-permute-start.12) | collective-permute-done | bytes 2097184 | tf_op jit(solution)/shard_map/ppermute | solution.py:18
  459.0 0.3 broadcast_select_fusion.6
  460.2 0.2 select_reduce_fusion.1
  460.6 26.5 %collective-permute-done.13 = f32[8,4,128,128]{2,3,0,1:T(8,128)} collective-permute-done((f32[8,4,128,128]{2,3,0,1:T(8,128)S(1)}, f32[8,4,128,128]{2,3,0,1:T(8,128)}, u32[]{:S(2)}, u32[]{:S(2)}) %collective-permute-start.13) | collective-permute-done | bytes 2097184 | tf_op jit(solution)/shard_map/ppermute | solution.py:18
  487.0 3.2 broadcast_select_fusion.7
  490.3 2.0 copy.35
  492.3 1.9 fusion.21
  494.2 13.0 %bitcast_add_fusion = f32[16,8,128,128]{3,1,2,0:T(8,128)S(1)} fusion(f32[16,1,8,1,128,128]{5,4,3,2,1,0:T(8,128)} %param.9, f32[16,4,128,128]{3,0,2,1:T(8,128)S(1)} %fusion.21, s32[4]{0:T(128)S(1)} %and_select_fusion), kind=kOutput, calls=%fused_computation.3 | convolution fusion | flops 102760480 | bytes 20971536 | tf_op jit(solution)/shard_map/bs,asxy->abxy/dot_general | solution.py:157
  507.2 1.3 broadcast.775
  508.5 5.8 broadcast_select_fusion
  514.3 1.1 select_bitcast_fusion.2
  515.4 1.6 select_bitcast_fusion
  517.0 0.2 all-reduce.7.cloned.1.call-start
  517.2 104.2 %all-reduce.9.cloned.1.call-done = (f32[16,128,128]{2,1,0:T(8,128)}, f32[16,128,128]{2,1,0:T(8,128)}, f32[16,128,128]{2,1,0:T(8,128)}, f32[16,128,128]{2,1,0:T(8,128)}) async-done(((f32[16,128,128]{2,1,0:T(8,128)}, f32[16,128,128]{2,1,0:T(8,128)}, f32[16,128,128]{2,1,0:T(8,128)}, f32[16,128,128]{2,1,0:T(8,128)}), (f32[16,128,128]{2,1,0:T(8,128)}, f32[16,128,128]{2,1,0:T(8,128)}, f32[16,128,128]{2,1,0:T(8,128)}, ...) | async-done | bytes 4194320 | tf_op jit(solution)/shard_map/psum | solution.py:13
  621.4 1.5 constant_dynamic-update-slice_fusion.3
  623.4 0.9 copy-done.5
  624.4 2.0 copy-done.2
  626.3 1.6 fusion.7
  628.1 9.9 %fusion.10 = f32[16,128,512]{2,1,0:T(8,128)} fusion(f32[16,128,512]{2,1,0:T(8,128)} %copy-done.2, f32[512,512]{1,0:T(8,128)S(1)} %copy-done), kind=kOutput, calls=%fused_computation.14 | convolution fusion | flops 6442450944 | bytes 9437184 | tf_op jit(solution)/shard_map/axp,pq->axq/dot_general | solution.py:169
  638.0 55.2 %all-reduce.7.cloned.1.call-done = f32[8,128,512]{2,1,0:T(8,128)} async-done(((f32[8,128,512]{2,1,0:T(8,128)}), f32[8,128,512]{2,1,0:T(8,128)}) %all-reduce.7.cloned.1.call-update) | async-done | bytes 2097168 | tf_op jit(solution)/shard_map/psum | solution.py:13
  693.1 18.0 %fusion.1 = f32[8,128,16,128]{3,1,2,0:T(8,128)} fusion(f32[16,128,512]{2,1,0:T(8,128)} %fusion.10, f32[8,128,512]{2,1,0:T(8,128)} %all-reduce.7.cloned.1.call-done), kind=kOutput, calls=%fused_computation.4 | convolution fusion | flops 12884901888 | bytes 14680064 | tf_op jit(solution)/shard_map/axq,byq->abxy/dot_general | solution.py:176
  711.2 9.4 %copy.42 = f32[8,128,16,128]{1,0,3,2:T(8,128)} copy(f32[8,128,16,128]{3,1,2,0:T(8,128)} %fusion.1) | data formatting | bytes 16777216 | tf_op jit(solution)/shard_map/axq,byq->abxy/dot_general | solution.py:176
  720.6 10.2 %fusion = f32[16,1,8,1,128,128]{5,2,4,0,3,1:T(8,128)} fusion(f32[16,8,128,128]{3,1,2,0:T(8,128)} %copy-done.1, f32[8,128,16,128]{1,0,3,2:T(8,128)} %copy.42, pred[16,8]{1,0:T(8,128)(4,1)S(1)} %compare_and_fusion), kind=kLoop, calls=%fused_computation.2 | loop fusion | flops 4194304 | bytes 25165952 | tf_op jit(solution)/shard_map/broadcast_in_dim | solution.py:183
  730.8 8.2 %copy.43 = f32[16,1,8,1,128,128]{5,4,3,2,1,0:T(8,128)} copy(f32[16,1,8,1,128,128]{5,2,4,0,3,1:T(8,128)} %fusion) | data formatting | bytes 16777216 | tf_op jit(solution)/shard_map/broadcast_in_dim | solution.py:183
  (62 shorter events, 1.8 us)
Async XLA Ops:
  7.4 620.7 %copy-start = (f32[512,512]{1,0:T(8,128)S(1)}, f32[512,512]{1,0:T(8,128)}, u32[]{:S(2)}) copy-start(f32[512,512]{1,0:T(8,128)} %param.15) | copy-start | bytes 3145732
  7.4 10.5 %copy-start.4 = (f32[8,1,64,128]{3,2,1,0:T(8,128)S(1)}, f32[8,1,64,128]{3,2,1,0:T(8,128)}, u32[]{:S(2)}) copy-start(f32[8,1,64,128]{3,2,1,0:T(8,128)} %param.11) | copy-start | bytes 786436
  7.4 162.1 %reduce-scatter.2.cloned.1.call-start = ((), (), s32[]{:S(2)}) async-start(), calls=%async_computation.2 | async-start | bytes 8912896 | tf_op jit(solution)/shard_map/reduce_scatter | solution.py:107
  7.4 7.3 collective-permute-start
  7.4 7.3 collective-permute-start.1
  14.7 7.3 collective-permute-start.2
  14.7 9.3 %collective-permute-start.3 = (f32[8,1,64,128]{3,2,1,0:T(8,128)}, f32[8,1,64,128]{3,2,1,0:T(8,128)}, u32[]{:S(2)}, u32[]{:S(2)}) collective-permute-start(f32[8,1,64,128]{3,2,1,0:T(8,128)} %collective-permute-done.1), channel_id=1, source_target_pairs={{0,112},{16,0},{32,16},{48,32},{64,48},{80,64},{96,80},{112,96},{1... | collective-permute-start | bytes 786440 | tf_op jit(solution)/shard_map/ppermute | solution.py:87
  22.0 7.2 collective-permute-start.4
  24.0 7.2 collective-permute-start.5
  29.2 7.0 collective-permute-start.6
  84.5 0.9 copy-start.8
  84.5 1.7 copy-start.9
  84.5 2.3 copy-start.3
  84.5 89.3 %all-reduce.5.cloned.1.call-start = ((), (), s32[]{:S(2)}) async-start(), calls=%async_computation.1 | async-start | bytes 262144 | tf_op jit(solution)/shard_map/psum | solution.py:13
  86.1 535.3 %all-reduce.9.cloned.1.call-start = ((), (), s32[]{:S(2)}) async-start(), calls=%async_computation.4 | async-start | bytes 8388608 | tf_op jit(solution)/shard_map/psum | solution.py:13
  173.8 4.0 copy-start.10
  177.7 26.8 %collective-permute-start.7 = (f32[8,4,128,128]{2,3,0,1:T(8,128)S(1)}, f32[8,4,128,128]{2,3,0,1:T(8,128)}, u32[]{:S(2)}, u32[]{:S(2)}) collective-permute-start(f32[8,4,128,128]{2,3,0,1:T(8,128)S(1)} %fusion.9), channel_id=1, source_target_pairs={{0,16},{16,32},{32,48},{48,64},{64,80},{80,96},{96,112},{112,0},{1... | collective-permute-start | bytes 6291464 | tf_op jit(solution)/shard_map/ppermute | solution.py:18
  206.4 46.6 %collective-permute-start.8 = (f32[8,4,128,128]{2,3,0,1:T(8,128)S(1)}, f32[8,4,128,128]{2,3,0,1:T(8,128)S(1)}, u32[]{:S(2)}, u32[]{:S(2)}) collective-permute-start(f32[8,4,128,128]{2,3,0,1:T(8,128)S(1)} %broadcast_select_fusion.1), channel_id=1, source_target_pairs={{0,32},{16,48},{32,64},{48,80},{64,96},{80,112},{96,0},{112,16},{1... | collective-permute-start | bytes 6291464 | tf_op jit(solution)/shard_map/ppermute | solution.py:18
  253.5 46.5 %collective-permute-start.9 = (f32[8,4,128,128]{2,3,0,1:T(8,128)S(1)}, f32[8,4,128,128]{2,3,0,1:T(8,128)S(1)}, u32[]{:S(2)}, u32[]{:S(2)}) collective-permute-start(f32[8,4,128,128]{2,3,0,1:T(8,128)S(1)} %broadcast_select_fusion.2), channel_id=1, source_target_pairs={{0,64},{16,80},{32,96},{48,112},{64,0},{80,16},{96,32},{112,48},{1... | collective-permute-start | bytes 6291464 | tf_op jit(solution)/shard_map/ppermute | solution.py:18
  300.4 47.7 %collective-permute-start.10 = (f32[8,4,128,128]{2,3,0,1:T(8,128)S(1)}, f32[8,4,128,128]{2,3,0,1:T(8,128)S(1)}, u32[]{:S(2)}, u32[]{:S(2)}) collective-permute-start(f32[8,4,128,128]{2,3,0,1:T(8,128)S(1)} %broadcast_select_fusion.3), channel_id=1, source_target_pairs={{0,1},{1,2},{2,3},{3,4},{4,5},{5,6},{6,7},{7,8},{8,9},{9,10},{10,1... | collective-permute-start | bytes 6291464 | tf_op jit(solution)/shard_map/ppermute | solution.py:18
  348.5 49.9 %collective-permute-start.11 = (f32[8,4,128,128]{2,3,0,1:T(8,128)S(1)}, f32[8,4,128,128]{2,3,0,1:T(8,128)S(1)}, u32[]{:S(2)}, u32[]{:S(2)}) collective-permute-start(f32[8,4,128,128]{2,3,0,1:T(8,128)S(1)} %broadcast_select_fusion.4), channel_id=1, source_target_pairs={{0,2},{1,3},{2,4},{3,5},{4,6},{5,7},{6,8},{7,9},{8,10},{9,11},{10,... | collective-permute-start | bytes 6291464 | tf_op jit(solution)/shard_map/ppermute | solution.py:18
  398.9 60.1 %collective-permute-start.12 = (f32[8,4,128,128]{2,3,0,1:T(8,128)S(1)}, f32[8,4,128,128]{2,3,0,1:T(8,128)S(1)}, u32[]{:S(2)}, u32[]{:S(2)}) collective-permute-start(f32[8,4,128,128]{2,3,0,1:T(8,128)S(1)} %broadcast_select_fusion.5), channel_id=1, source_target_pairs={{0,4},{1,5},{2,6},{3,7},{4,8},{5,9},{6,10},{7,11},{8,12},{9,13},{1... | collective-permute-start | bytes 6291464 | tf_op jit(solution)/shard_map/ppermute | solution.py:18
  459.3 27.7 %collective-permute-start.13 = (f32[8,4,128,128]{2,3,0,1:T(8,128)S(1)}, f32[8,4,128,128]{2,3,0,1:T(8,128)}, u32[]{:S(2)}, u32[]{:S(2)}) collective-permute-start(f32[8,4,128,128]{2,3,0,1:T(8,128)S(1)} %broadcast_select_fusion.6), channel_id=1, source_target_pairs={{0,8},{1,9},{2,10},{3,11},{4,12},{5,13},{6,14},{7,15},{8,0},{9,1},... | collective-permute-start | bytes 6291464 | tf_op jit(solution)/shard_map/ppermute | solution.py:18
  507.2 7.1 copy-start.1
  517.0 176.2 %all-reduce.7.cloned.1.call-start = ((), (), s32[]{:S(2)}) async-start(), calls=%async_computation.3 | async-start | bytes 4194304 | tf_op jit(solution)/shard_map/psum | solution.py:13
  621.4 1.5 copy-start.7
  621.4 1.9 copy-start.6
  622.9 1.3 copy-start.5
  624.4 2.0 copy-start.2
Sparse Core Ops, SparseCore 0:
  84.6 84.7 reduce-scatter.1
  517.1 104.2 all-reduce.8
Sparse Core Ops, SparseCore 1:
  87.3 60.4 all-reduce.4
  628.1 65.0 all-reduce.6
